TPU v7x, 128 devices: a whole 4x4x4 slice. The times are simulated.
128 devices in a mesh: bin: 16 (over z_lo, x, core), trk: 8 (over y, z_hi).
Axes of the slice: x: 4, y: 4, z: 4 (z_hi: 2, z_lo: 2; z = z_hi * 2 + z_lo), core: 2. Of those that a mesh axis runs over, the one named last changes fastest.
Arguments:
- trunk: bfloat16 [8192, 1536], P(('bin', 'trk')), may hold values from -6 to 6
- norm_gain: float32 [1536], replicated, may hold values from 0.1 to 1.9
- w_query: bfloat16 [1536, 1024], replicated, may hold values from -0.4375 to 0.4375
- w_kv: bfloat16 [1536, 256], replicated, may hold values from -0.15625 to 0.15625
- w_out: bfloat16 [1024, 1536], replicated, may hold values from -0.1875 to 0.1875
- w_up: bfloat16 [1536, 768], replicated, may hold values from -0.15625 to 0.15625
- skip: bfloat16 [32768, 768], P(('bin', 'trk')), may hold values from -6 to 6
- conv_w: bfloat16 [5, 768, 768], replicated, may hold values from -0.09375 to 0.09375
- head_w: bfloat16 [768, 6144], P(None, 'trk'), may hold values from -0.21875 to 0.21875
- head_bias: float32 [6144], P('trk'), may hold values from -4 to 4
- targets: bfloat16 [32768, 6144], P('bin', 'trk'), may hold values from 0.049804688 to 4
- missing: int32 [8192], P('bin'), may hold values 0 or 1
- group_ids: int32 [6144, 1], replicated, may hold values from 0 to 10
- group_weight: float32 [11], replicated, may hold values from 0.25 to 4
Outputs:
- prediction: bfloat16 [32768, 6144], P('bin', 'trk')
- head_grad: float32 [768, 6144], P('bin', 'trk')
- feature_grad: bfloat16 [32768, 768], P(('bin', 'trk'))
Inputs may be any that keep to these rules, and one draw needn't show every extreme that they name: `group_ids`: every group id is held by at least one track.
All inputs are finite; a program needn't handle non-finite values. No bound on the sum of `missing` on one device may be relied on, other than what follows from the above.
Results may differ from a plain program's by a relative error of at most 0.019.
Values may be sent and summed in bfloat16 or wider, within the bound.
No kernel may reach another device: no remote copies, remote signals or barrier semaphores. Data moves between devices by JAX's collectives and lax.ppermute only.
A program may use at most 128 MiB of HBM per device.

v0:
```python
import math
import jax
import jax.numpy as jnp
from jax import lax
from jax.sharding import PartitionSpec as P

logit_cap = 20.0


def padded_2(value, sides, width):
    for axis, dim in sides:
        size, length = (lax.axis_size(axis), value.shape[dim])
        up = [(i, (i + 1) % size) for i in range(size - 1)]
        down = [(j, i) for i, j in up]
        last = lax.slice_in_dim(value, length - width, length, axis=dim)
        initial = lax.slice_in_dim(value, 0, width, axis=dim)
        before = lax.ppermute(last, axis, up)
        after = lax.ppermute(initial, axis, down)
        value = jnp.concatenate([before, value, after], axis=dim)
    return value


def attend_block(state_pair, queries, key_block, value_block, score_scale):
    numerator, denominator = state_pair
    scores = (
        jnp.einsum("rhd,nd->rhn", queries, key_block, preferred_element_type=jnp.float32)
        * score_scale
    )
    scores = logit_cap * jnp.tanh(scores / logit_cap)
    exp_weights = jnp.exp(scores)
    numerator = numerator + jnp.einsum(
        "rhn,nd->rhd",
        exp_weights.astype(jnp.bfloat16),
        value_block,
        preferred_element_type=jnp.float32,
    )
    denominator = denominator + jnp.sum(exp_weights, axis=2)
    return (numerator, denominator)


def make_folder(queries, head_dim):
    score_scale = 1.0 / math.sqrt(head_dim)

    def fold(accum, key_piece, offset):
        piece_rows = key_piece.shape[0]
        block_rows = math.gcd(piece_rows, 2048)
        stacked = key_piece.reshape(piece_rows // block_rows, block_rows, key_piece.shape[1])

        def fold_step(running, one_block):
            updated = attend_block(
                running, queries, one_block[:, :head_dim], one_block[:, head_dim:], score_scale
            )
            return (updated, None)

        result, _ = lax.scan(fold_step, accum, stacked)
        return result

    return fold


def body(
    trunk,
    norm_gain,
    w_query,
    w_kv,
    w_out,
    w_up,
    skip,
    conv_w,
    head_w,
    head_bias,
    targets,
    missing,
    group_ids,
    group_weight,
):
    row_count = trunk.shape[0]
    head_dim = w_kv.shape[1] // 2
    head_count = w_query.shape[1] // head_dim
    widened = trunk.astype(jnp.float32)
    meansq = jnp.mean(widened * widened, axis=1, keepdims=True)
    normed = (widened * lax.rsqrt(meansq + 1e-06) * norm_gain).astype(jnp.bfloat16)
    queries = (
        jnp.dot(normed, w_query, preferred_element_type=jnp.float32)
        .astype(jnp.bfloat16)
        .reshape(row_count, head_count, head_dim)
    )
    keyvals = jnp.dot(normed, w_kv, preferred_element_type=jnp.float32).astype(jnp.bfloat16)
    start_pair = (
        jnp.zeros((row_count, head_count, head_dim), jnp.float32),
        jnp.zeros((row_count, head_count), jnp.float32),
    )
    folder = make_folder(queries, head_dim)
    numerator, denominator = folder(
        start_pair, lax.all_gather(keyvals, ("bin", "trk"), axis=0, tiled=True), jnp.int32(0)
    )
    attended = (
        (numerator / denominator[:, :, None])
        .astype(jnp.bfloat16)
        .reshape(row_count, head_count * head_dim)
    )
    hidden = (widened + jnp.dot(attended, w_out, preferred_element_type=jnp.float32)).astype(
        jnp.bfloat16
    )
    upward = jnp.dot(hidden, w_up, preferred_element_type=jnp.float32)
    factor = skip.shape[0] // row_count
    upsampled = (jnp.repeat(upward, factor, axis=0) + skip.astype(jnp.float32)).astype(jnp.bfloat16)
    tap_count = conv_w.shape[0]
    rim_width = tap_count // 2
    padded = padded_2(upsampled, ((("bin", "trk"), 0),), rim_width)
    pos_count = upsampled.shape[0]
    windows = jnp.concatenate([padded[tap : tap + pos_count] for tap in range(tap_count)], axis=1)
    kernel_flat = conv_w.reshape(tap_count * conv_w.shape[1], conv_w.shape[2])
    conved = jnp.dot(windows, kernel_flat, preferred_element_type=jnp.float32)
    feature = (upsampled.astype(jnp.float32) + jax.nn.gelu(conved)).astype(jnp.bfloat16)
    panel_feat = lax.all_gather(feature, "trk", axis=0, tiled=True)
    logits = jnp.dot(panel_feat, head_w, preferred_element_type=jnp.float32) + head_bias
    smooth = jax.nn.softplus(logits)
    prediction = smooth.astype(jnp.bfloat16)
    tile_width = head_w.shape[1]
    groups = group_weight.shape[0]
    total_tracks = group_ids.shape[0]
    labels = jnp.arange(groups, dtype=jnp.int32)
    counts = jnp.sum((group_ids == labels[None, :]).astype(jnp.int32), axis=0)
    per_group = group_weight * total_tracks / (groups * counts.astype(jnp.float32))
    local_ids = lax.dynamic_slice_in_dim(
        group_ids, lax.axis_index("trk") * tile_width, tile_width, 0
    )
    track_scale = jnp.sum(jnp.where(local_ids == labels[None, :], per_group[None, :], 0.0), axis=1)
    keep_mask = 1.0 - jnp.repeat(missing.astype(jnp.float32), factor)[:, None]
    misfit = smooth - targets.astype(jnp.float32)
    slope_grad = (keep_mask * track_scale[None, :] * misfit * jax.nn.sigmoid(logits)).astype(
        jnp.bfloat16
    )
    positions = panel_feat.shape[0] * lax.axis_size("bin")
    product = lax.dot_general(
        panel_feat, slope_grad, (((0,), (0,)), ((), ())), preferred_element_type=jnp.float32
    )
    head_grad = lax.psum_scatter(
        (product / positions).astype(jnp.bfloat16), "bin", scatter_dimension=0, tiled=True
    ).astype(jnp.float32)
    partial_value = lax.dot_general(
        slope_grad, head_w, (((1,), (1,)), ((), ())), preferred_element_type=jnp.float32
    )
    feature_grad = lax.psum_scatter(
        partial_value.astype(jnp.bfloat16), "trk", scatter_dimension=0, tiled=True
    )
    return (prediction, head_grad, feature_grad)


def solution(mesh):
    in_specs = (
        P(("bin", "trk"), None),
        P(),
        P(),
        P(),
        P(),
        P(),
        P(("bin", "trk"), None),
        P(),
        P(None, "trk"),
        P("trk"),
        P("bin", "trk"),
        P("bin"),
        P(),
        P(),
    )
    out_specs = (P("bin", "trk"), P("bin", "trk"), P(("bin", "trk"), None))
    return jax.shard_map(body, mesh=mesh, in_specs=in_specs, out_specs=out_specs, check_vma=False)
```

profile of v0, /device:TPU:0, one launch (start us, length us, event | category | flops | bytes accessed | tf_op | source)
XLA Modules:
  0.0 599.8 jit_solution(18380595523179321211)
XLA Ops:
  7.2 0.0 copy-start
  7.2 0.0 all-gather.3.cloned.1.call-start
  7.2 1.2 fusion.20
  8.5 2.2 convolution_convert_fusion.2
  10.6 0.0 all-gather.3.cloned.1.call-update
  10.7 0.0 all-gather.5.cloned.1.call-start
  10.7 0.0 copy-done
  10.7 1.6 fusion.5
  12.4 306.4 %all-gather.3.cloned.1.call-done = bf16[8192,256]{1,0:T(8,128)(2,1)} async-done(((bf16[64,256]{1,0:T(8,128)(2,1)}), bf16[8192,256]{1,0:T(8,128)(2,1)}) %all-gather.3.cloned.1.call-update) | async-done | bytes 4194320 | tf_op jit(solution)/shard_map/all_gather | solution.py:95
  318.8 22.4 %while.15 = (s32[]{:T(128)}, f32[64,8,128]{2,0,1:T(8,128)S(1)}, f32[64,8]{0,1:T(8,128)S(1)}, bf16[4,2048,256]{2,1,0:T(8,128)(2,1)}, bf16[64,8,128]{2,0,1:T(8,128)(2,1)S(1)}, /*index=5*/s32[]{:T(128)}, s32[]{:T(128)}) while((s32[]{:T(128)}, f32[64,8,128]{2,0,1:T(8,128)S(1)}, f32[64,8]{0,1:T(8,128)S(1)}, ...), condition=%wide.region_3.4_spmd.clone, body=%wide.region_1.3_spmd.clone.sunk | while | flops 541196800 | bytes 12198016 | solution.py:55
  318.8 2.3 dynamic-slice_bitcast_fusion.2
  321.1 2.5 bitcast_reduce_fusion.2
  323.6 0.0 copy-done.1
  323.6 0.8 fusion.56
  324.4 2.3 dynamic-slice_bitcast_fusion.2
  326.7 2.5 bitcast_reduce_fusion.2
  329.2 0.0 copy-done.1
  329.2 0.8 fusion.56
  330.0 2.3 dynamic-slice_bitcast_fusion.2
  332.3 2.5 bitcast_reduce_fusion.2
  334.8 0.0 copy-done.1
  334.8 0.8 fusion.56
  335.6 2.3 dynamic-slice_bitcast_fusion.2
  337.9 2.5 bitcast_reduce_fusion.2
  340.4 0.0 copy-done.1
  340.4 0.8 fusion.56
  341.2 4.4 fusion.4
  345.7 1.9 broadcast_in_dim.34
  347.6 2.3 reshape.46
  349.9 1.3 add_convert_fusion
  351.2 4.5 collective-permute-start
  355.7 1.3 collective-permute-start.1
  357.0 0.0 collective-permute-done
  357.1 0.1 fusion.19
  357.2 0.1 fusion.24
  357.3 5.4 collective-permute-done.1
  362.7 0.1 fusion.17
  362.8 0.1 fusion.23
  363.0 0.0 copy-start.3
  363.0 0.0 copy-start.2
  363.0 0.0 copy-start.6
  363.0 0.0 copy-start.5
  363.0 5.3 fusion.14
  368.3 0.0 all-gather.5.cloned.1.call-update
  368.3 0.2 reduce-scatter.3.cloned.1.call-start
  368.5 0.0 copy-done.3
  368.6 0.1 broadcast_in_dim.35
  368.7 0.2 sub.20
  368.9 0.0 copy-done.2
  368.9 0.2 convert_reduce_fusion
  369.1 0.0 copy-done.6
  369.1 0.1 select_reduce_fusion
  369.2 65.0 %all-gather.5.cloned.1.call-done = bf16[2048,768]{1,0:T(8,128)(2,1)} async-done(((bf16[256,768]{1,0:T(8,128)(2,1)}), bf16[2048,768]{1,0:T(8,128)(2,1)}) %all-gather.5.cloned.1.call-update) | async-done | bytes 3145744 | tf_op jit(solution)/shard_map/all_gather | solution.py:116
  434.2 0.0 copy-done.5
  434.2 10.5 %multiply_convert_fusion = (bf16[2048,768]{1,0:T(8,128)(2,1)S(1)}, bf16[2048,768]{1,0:T(8,128)(2,1)}) fusion(bf16[2048,768]{1,0:T(8,128)(2,1)} %param.26, f32[768]{0:T(1024)S(1)} %select_reduce_fusion, f32[2048]{0:T(1024)S(1)} %sub.20, f32[768]{0:T(1024)S(1)} %copy-done.5, bf16[2048,768]{1,0:T(8,128)(2,1)} %all-gather.5.cloned.1.call-done, ...), kind=kOutput, calls=%fused_computation.10 | convolution fusion | flops 2442657792 | bytes 13776896 | tf_op jit(solution)/shard_map/dot_general | solution.py:117
  444.7 1.7 copy-done.7
  446.4 3.7 multiply_convert_fusion.1
  450.1 0.0 reduce-scatter.3.cloned.1.call-update
  450.1 0.0 reduce-scatter.5.cloned.1.call-start
  450.2 6.5 %convolution_convert_fusion = bf16[2048,768]{1,0:T(8,128)(2,1)} fusion(bf16[2048,768]{1,0:T(8,128)(2,1)} %copy-done.7, bf16[768,768]{1,0:T(8,128)(2,1)} %param.24), kind=kOutput, calls=%fused_computation.12 | convolution fusion | flops 2417491968 | bytes 7471104 | tf_op jit(solution)/shard_map/dot_general | solution.py:142
  456.7 0.0 reduce-scatter.5.cloned.1.call-update
  456.7 53.6 %reduce-scatter.3.cloned.1.call-done = bf16[48,768]{1,0:T(8,128)(2,1)} async-done(((bf16[768,768]{1,0:T(8,128)(2,1)}), bf16[48,768]{1,0:T(8,128)(2,1)}) %reduce-scatter.3.cloned.1.call-update) | async-done | bytes 73744 | tf_op jit(solution)/shard_map/reduce_scatter | solution.py:139
  510.4 1.6 convert_element_type.80
  511.9 81.4 %reduce-scatter.5.cloned.1.call-done = bf16[256,768]{1,0:T(8,128)(2,1)} async-done(((bf16[2048,768]{1,0:T(8,128)(2,1)}), bf16[256,768]{1,0:T(8,128)(2,1)}) %reduce-scatter.5.cloned.1.call-update) | async-done | bytes 393232 | tf_op jit(solution)/shard_map/reduce_scatter | solution.py:145
  (20 shorter events, 0.1 us)
Async XLA Ops:
  7.2 3.6 copy-start
  7.2 311.6 %all-gather.3.cloned.1.call-start = ((), (), s32[]{:S(2)}) async-start(), calls=%async_computation.2 | async-start | bytes 4227072 | tf_op jit(solution)/shard_map/all_gather | solution.py:95
  10.7 423.5 %all-gather.5.cloned.1.call-start = ((), (), s32[]{:S(2)}) async-start(), calls=%async_computation.3 | async-start | bytes 3538944 | tf_op jit(solution)/shard_map/all_gather | solution.py:116
  321.1 2.5 copy-start.1
  326.7 2.5 copy-start.1
  332.3 2.5 copy-start.1
  337.9 2.5 copy-start.1
  351.2 5.8 collective-permute-start
  355.7 7.0 %collective-permute-start.1 = (bf16[2,768]{1,0:T(2,128)(2,1)S(1)}, bf16[2,768]{1,0:T(2,128)(2,1)S(1)}, u32[]{:S(2)}, u32[]{:S(2)}) collective-permute-start(bf16[2,768]{1,0:T(2,128)(2,1)S(1)} %get-tuple-element.123), channel_id=1, source_target_pairs={{1,0},{2,1},{3,2},{4,3},{5,4},{6,5},{7,6},{8,7},{9,8},{10,9},{11,1... | collective-permute-start | bytes 9224 | tf_op jit(solution)/shard_map/ppermute | solution.py:18
  363.0 5.6 copy-start.3
  363.0 5.9 copy-start.2
  363.0 6.1 %copy-start.6 = (f32[11]{0:T(128)S(1)}, f32[11]{0:T(128)}, u32[]{:S(2)}) copy-start(f32[11]{0:T(128)} %param.29) | copy-start | bytes 136
  363.0 71.2 %copy-start.5 = (f32[768]{0:T(1024)S(1)}, f32[768]{0:T(1024)}, u32[]{:S(2)}) copy-start(f32[768]{0:T(1024)} %param.25) | copy-start | bytes 9220
  368.3 142.1 %reduce-scatter.3.cloned.1.call-start = ((), (), s32[]{:S(2)}) async-start(), calls=%async_computation.4 | async-start | bytes 1253376 | tf_op jit(solution)/shard_map/reduce_scatter | solution.py:139
  434.2 12.2 %copy-start.4 = (bf16[2048,768]{1,0:T(8,128)(2,1)S(1)}, bf16[2048,768]{1,0:T(8,128)(2,1)}, u32[]{:S(2)}) copy-start(bf16[2048,768]{1,0:T(8,128)(2,1)} %all-gather.5.cloned.1.call-done) | copy-start | bytes 9437188
  444.7 1.7 copy-start.7
  450.1 143.2 %reduce-scatter.5.cloned.1.call-start = ((), (), s32[]{:S(2)}) async-start(), calls=%async_computation.5 | async-start | bytes 3538944 | tf_op jit(solution)/shard_map/reduce_scatter | solution.py:145
Sparse Core Ops, SparseCore 0:
  10.8 307.9 all-gather.2
  368.4 65.7 all-gather.4
  450.2 60.0 reduce-scatter.2
  514.7 78.5 reduce-scatter.4
where the time goes:
time: 600 us
  waiting for transfers between devices  512 us (85%)
  matrix products  47.5 us (8%)
  local copies, waits for them, and re-layouts  15.4 us (3%)
  between operations  14 us (2%)
  starting transfers between devices  6.16 us (1%)
    all_gather x1, waiting for transfers between devices, body(): lax.all_gather(keyvals, ('bin', 'trk'), axis=0, tiled=True)  306 us
    reduce_scatter x1, waiting for transfers between devices, body(): lax.psum_scatter(partial_value.astype(jnp.bfloat16), 'trk', scatter_dimen...  81.4 us
    all_gather x1, waiting for transfers between devices, body(): panel_feat = lax.all_gather(feature, 'trk', axis=0, tiled=True)  65 us
    reduce_scatter x1, waiting for transfers between devices, body(): lax.psum_scatter((product / positions).astype(jnp.bfloat16), 'bin', scatt...  53.6 us
  transfers between devices with their start and end apart: 6, of which 5 were waited for; matrix products, arithmetic and copies ran while one was open for 2% of the time, Pallas kernels for 0%

commit v1 on v0

--- a/solution.py
+++ b/solution.py
@@ -92,7 +92,14 @@
     )
     folder = make_folder(queries, head_dim)
     numerator, denominator = folder(
-        start_pair, lax.all_gather(keyvals, ("bin", "trk"), axis=0, tiled=True), jnp.int32(0)
+        start_pair,
+        jnp.concatenate(
+            lax.all_to_all(
+                jnp.stack([keyvals] * lax.axis_size(("bin", "trk"))), ("bin", "trk"), 0, 0
+            ),
+            axis=0,
+        ),
+        jnp.int32(0),
     )
     attended = (
         (numerator / denominator[:, :, None])

time: 600 us -> 354 us (0.59)
  waiting for transfers between devices: 512 us -> 252 us
  starting transfers between devices: 6.16 us -> 18.2 us
    all_gather x1 -> x0, waiting for transfers between devices: 306 us -> none  [body(): lax.all_gather(keyvals, ('bin', 'trk'), axis=0, tiled=True)]
    all_to_all x0 -> x1, waiting for transfers between devices: none -> 48.4 us  [body(): lax.all_to_all(jnp.stack([keyvals] * lax.axis_size(('bin', 'trk'))), ('bi...]
    all_to_all x0 -> x1, starting transfers between devices: none -> 11.7 us  [body(): lax.all_to_all(jnp.stack([keyvals] * lax.axis_size(('bin', 'trk'))), ('bi...]
  transfers between devices with their start and end apart: 6 -> 6, of which waited for: 5 -> 5; matrix products, arithmetic and copies ran while one was open for 2% -> 3% of each run, Pallas kernels for 0% -> 0%
where the time goes in v1:
time: 354 us
  waiting for transfers between devices  252 us (71%)
  matrix products  46.9 us (13%)
  starting transfers between devices  18.2 us (5%)
  local copies, waits for them, and re-layouts  17.9 us (5%)
  between operations  14 us (4%)
  other arithmetic  4.76 us (1%)
    reduce_scatter x1, waiting for transfers between devices, body(): lax.psum_scatter(partial_value.astype(jnp.bfloat16), 'trk', scatter_dimen...  81.5 us
    all_gather x1, waiting for transfers between devices, body(): panel_feat = lax.all_gather(feature, 'trk', axis=0, tiled=True)  62.9 us
    reduce_scatter x1, waiting for transfers between devices, body(): lax.psum_scatter((product / positions).astype(jnp.bfloat16), 'bin', scatt...  53.6 us
    all_to_all x1, waiting for transfers between devices, body(): lax.all_to_all(jnp.stack([keyvals] * lax.axis_size(('bin', 'trk'))), ('bi...  48.4 us
    all_to_all x1, starting transfers between devices, body(): lax.all_to_all(jnp.stack([keyvals] * lax.axis_size(('bin', 'trk'))), ('bi...  11.7 us
    dot_general x1, matrix products, body(): jnp.dot(panel_feat, head_w, preferred_element_type=jnp.float32) + head_bias  10.5 us
    dot_general x4, matrix products, attend_block(): jnp.einsum('rhd,nd->rhn', queries, key_block, preferred_element_type=jnp....  10.2 us
    squeeze x4, local copies, waits for them, and re-layouts, fold(): result, _ = lax.scan(fold_step, accum, stacked)  9.06 us
  transfers between devices with their start and end apart: 6, of which 5 were waited for; matrix products, arithmetic and copies ran while one was open for 3% of the time, Pallas kernels for 0%

profile of v1, /device:TPU:0, one launch (start us, length us, event | category | flops | bytes accessed | tf_op | source)
XLA Modules:
  0.0 353.7 jit_solution(3387256162302402909)
XLA Ops:
  7.2 0.0 copy-start
  7.2 1.2 fusion.20
  8.4 1.6 convolution_convert_fusion.2
  10.0 2.5 stack.2
  12.5 11.7 %all-to-all-start = ((bf16[128,64,256]{2,1,0:T(8,128)(2,1)}), bf16[128,64,256]{2,1,0:T(8,128)(2,1)}, u32[]{:S(2)}, u32[]{:S(2)}) async-start(bf16[128,64,256]{2,1,0:T(8,128)(2,1)} %stack.2), calls=%async_computation | async-start | bytes 8388608 | tf_op jit(solution)/shard_map/all_to_all | solution.py:97
  24.2 0.0 all-gather.2.cloned.1.call-start
  24.2 0.0 copy-done
  24.2 0.0 copy-done.2
  24.3 1.6 fusion.5
  25.9 48.4 %all-to-all-done = bf16[128,64,256]{2,1,0:T(8,128)(2,1)} async-done(((bf16[128,64,256]{2,1,0:T(8,128)(2,1)}), bf16[128,64,256]{2,1,0:T(8,128)(2,1)}, u32[]{:S(2)}, u32[]{:S(2)}) %all-to-all-start) | async-done | bytes 4194336 | tf_op jit(solution)/shard_map/all_to_all | solution.py:97
  74.3 22.4 %while.15 = (s32[]{:T(128)}, f32[64,8,128]{2,0,1:T(8,128)S(1)}, f32[64,8]{0,1:T(8,128)S(1)}, bf16[4,2048,256]{2,1,0:T(8,128)(2,1)}, bf16[64,8,128]{2,0,1:T(8,128)(2,1)S(1)}, /*index=5*/s32[]{:T(128)}, s32[]{:T(128)}) while((s32[]{:T(128)}, f32[64,8,128]{2,0,1:T(8,128)S(1)}, f32[64,8]{0,1:T(8,128)S(1)}, ...), condition=%wide.region_3.4_spmd.clone, body=%wide.region_1.3_spmd.clone.sunk | while | flops 541196800 | bytes 12198016 | solution.py:55
  74.3 2.3 dynamic-slice_bitcast_fusion.2
  76.6 2.5 bitcast_reduce_fusion.2
  79.1 0.0 copy-done.1
  79.1 0.8 fusion.56
  79.9 2.3 dynamic-slice_bitcast_fusion.2
  82.2 2.5 bitcast_reduce_fusion.2
  84.7 0.0 copy-done.1
  84.7 0.8 fusion.56
  85.5 2.3 dynamic-slice_bitcast_fusion.2
  87.8 2.5 bitcast_reduce_fusion.2
  90.3 0.0 copy-done.1
  90.3 0.8 fusion.56
  91.1 2.3 dynamic-slice_bitcast_fusion.2
  93.4 2.5 bitcast_reduce_fusion.2
  95.9 0.0 copy-done.1
  95.9 0.8 fusion.56
  96.7 4.4 %fusion.4 = f32[64,768]{1,0:T(8,128)} fusion(bf16[1536,768]{1,0:T(8,128)(2,1)} %param.21, bf16[1024,1536]{1,0:T(8,128)(2,1)} %param.20, bf16[64,1536]{1,0:T(8,128)(2,1)} %param.16, f32[64,8,128]{2,0,1:T(8,128)S(1)} %get-tuple-element.69, f32[64,8]{0,1:T(8,128)S(1)} %get-tuple-element.70), kind=kOutput, calls=%fused_computation.17 | convolution fusion | flops 352747520 | bytes 6162432 | tf_op jit(solution)/shard_map/dot_general | solution.py:112
  101.2 1.9 broadcast_in_dim.34
  103.1 2.3 reshape.44
  105.4 1.3 add_convert_fusion
  106.7 4.9 %collective-permute-start = (bf16[2,768]{1,0:T(2,128)(2,1)S(1)}, bf16[2,768]{1,0:T(2,128)(2,1)S(1)}, u32[]{:S(2)}, u32[]{:S(2)}) collective-permute-start(bf16[2,768]{1,0:T(2,128)(2,1)S(1)} %get-tuple-element.124), channel_id=1, source_target_pairs={{0,1},{1,2},{2,3},{3,4},{4,5},{5,6},{6,7},{7,8},{8,9},{9,10},{10,1... | collective-permute-start | bytes 9224 | tf_op jit(solution)/shard_map/ppermute | solution.py:17
  111.6 1.3 collective-permute-start.1
  112.9 0.0 collective-permute-done
  112.9 0.1 fusion.19
  113.0 0.1 fusion.24
  113.2 5.4 %collective-permute-done.1 = bf16[2,768]{1,0:T(2,128)(2,1)S(1)} collective-permute-done((bf16[2,768]{1,0:T(2,128)(2,1)S(1)}, bf16[2,768]{1,0:T(2,128)(2,1)S(1)}, u32[]{:S(2)}, u32[]{:S(2)}) %collective-permute-start.1) | collective-permute-done | bytes 3104 | tf_op jit(solution)/shard_map/ppermute | solution.py:18
  118.6 0.1 fusion.17
  118.7 0.1 fusion.23
  118.8 0.0 copy-start.4
  118.8 0.0 copy-start.3
  118.9 0.0 copy-start.7
  118.9 0.0 copy-start.6
  118.9 5.3 %fusion.14 = bf16[256,768]{1,0:T(8,128)(2,1)} fusion(bf16[256,768]{1,0:T(8,128)(2,1)S(1)} %add_convert_fusion, bf16[256,3840]{1,0:T(8,128)(2,1)S(1)} %fusion.23, bf16[3840,768]{1,0:T(8,128)(2,1)} %bitcast.63), kind=kOutput, calls=%fused_computation.29 | convolution fusion | flops 1512112128 | bytes 8650752 | tf_op jit(solution)/shard_map/dot_general | solution.py:121
  124.2 0.0 all-gather.2.cloned.1.call-update
  124.2 0.2 reduce-scatter.3.cloned.1.call-start
  124.4 0.0 copy-done.4
  124.5 0.1 broadcast_in_dim.35
  124.6 0.2 sub.20
  124.7 0.0 copy-done.3
  124.8 0.2 convert_reduce_fusion
  124.9 0.0 copy-done.7
  125.0 0.1 select_reduce_fusion
  125.1 62.9 %all-gather.2.cloned.1.call-done = bf16[2048,768]{1,0:T(8,128)(2,1)} async-done(((bf16[256,768]{1,0:T(8,128)(2,1)}), bf16[2048,768]{1,0:T(8,128)(2,1)}) %all-gather.2.cloned.1.call-update) | async-done | bytes 3145744 | tf_op jit(solution)/shard_map/all_gather | solution.py:123
  188.0 10.5 %multiply_convert_fusion = (bf16[2048,768]{1,0:T(8,128)(2,1)S(1)}, bf16[2048,768]{1,0:T(8,128)(2,1)}) fusion(bf16[2048,768]{1,0:T(8,128)(2,1)} %param.26, f32[768]{0:T(1024)S(1)} %select_reduce_fusion, f32[2048]{0:T(1024)S(1)} %sub.20, f32[768]{0:T(1024)S(1)} %copy-done.6, bf16[2048,768]{1,0:T(8,128)(2,1)} %all-gather.2.cloned.1.call-done, ...), kind=kOutput, calls=%fused_computation.10 | convolution fusion | flops 2442657792 | bytes 13776896 | tf_op jit(solution)/shard_map/dot_general | solution.py:124
  198.5 1.7 copy-done.8
  200.1 3.7 %multiply_convert_fusion.1 = bf16[768,768]{1,0:T(8,128)(2,1)} fusion(bf16[2048,768]{1,0:T(8,128)(2,1)S(1)} %copy-done.5, bf16[2048,768]{1,0:T(8,128)(2,1)S(1)} %get-tuple-element.121), kind=kOutput, calls=%fused_computation.13 | convolution fusion | flops 2417098752 | bytes 7471104 | tf_op jit(solution)/shard_map/dot_general | solution.py:143
  203.8 0.0 reduce-scatter.3.cloned.1.call-update
  203.9 0.0 reduce-scatter.5.cloned.1.call-start
  203.9 6.5 %convolution_convert_fusion = bf16[2048,768]{1,0:T(8,128)(2,1)} fusion(bf16[2048,768]{1,0:T(8,128)(2,1)} %copy-done.8, bf16[768,768]{1,0:T(8,128)(2,1)} %param.24), kind=kOutput, calls=%fused_computation.12 | convolution fusion | flops 2417491968 | bytes 7471104 | tf_op jit(solution)/shard_map/dot_general | solution.py:149
  210.5 0.0 reduce-scatter.5.cloned.1.call-update
  210.5 53.6 %reduce-scatter.3.cloned.1.call-done = bf16[48,768]{1,0:T(8,128)(2,1)} async-done(((bf16[768,768]{1,0:T(8,128)(2,1)}), bf16[48,768]{1,0:T(8,128)(2,1)}) %reduce-scatter.3.cloned.1.call-update) | async-done | bytes 73744 | tf_op jit(solution)/shard_map/reduce_scatter | solution.py:146
  264.1 1.6 convert_element_type.80
  265.6 81.5 %reduce-scatter.5.cloned.1.call-done = bf16[256,768]{1,0:T(8,128)(2,1)} async-done(((bf16[2048,768]{1,0:T(8,128)(2,1)}), bf16[256,768]{1,0:T(8,128)(2,1)}) %reduce-scatter.5.cloned.1.call-update) | async-done | bytes 393232 | tf_op jit(solution)/shard_map/reduce_scatter | solution.py:152
  (22 shorter events, 0.1 us)
Async XLA Ops:
  7.2 17.1 %copy-start = (bf16[1536,1024]{1,0:T(8,128)(2,1)S(1)}, bf16[1536,1024]{1,0:T(8,128)(2,1)}, u32[]{:S(2)}) copy-start(bf16[1536,1024]{1,0:T(8,128)(2,1)} %param.18) | copy-start | bytes 9437188
  12.5 11.8 %copy-start.2 = (f32[1536]{0:T(1024)S(1)}, f32[1536]{0:T(1024)}, u32[]{:S(2)}) copy-start(f32[1536]{0:T(1024)} %param.17) | copy-start | bytes 18436
  12.5 61.8 %all-to-all-start = ((bf16[128,64,256]{2,1,0:T(8,128)(2,1)}), bf16[128,64,256]{2,1,0:T(8,128)(2,1)}, u32[]{:S(2)}, u32[]{:S(2)}) async-start(bf16[128,64,256]{2,1,0:T(8,128)(2,1)} %stack.2), calls=%async_computation | async-start | bytes 8388608 | tf_op jit(solution)/shard_map/all_to_all | solution.py:97
  24.2 163.8 %all-gather.2.cloned.1.call-start = ((), (), s32[]{:S(2)}) async-start(), calls=%async_computation.3 | async-start | bytes 3538944 | tf_op jit(solution)/shard_map/all_gather | solution.py:123
  76.6 2.6 copy-start.1
  82.2 2.5 copy-start.1
  87.8 2.5 copy-start.1
  93.4 2.5 copy-start.1
  106.7 6.2 %collective-permute-start = (bf16[2,768]{1,0:T(2,128)(2,1)S(1)}, bf16[2,768]{1,0:T(2,128)(2,1)S(1)}, u32[]{:S(2)}, u32[]{:S(2)}) collective-permute-start(bf16[2,768]{1,0:T(2,128)(2,1)S(1)} %get-tuple-element.124), channel_id=1, source_target_pairs={{0,1},{1,2},{2,3},{3,4},{4,5},{5,6},{6,7},{7,8},{8,9},{9,10},{10,1... | collective-permute-start | bytes 9224 | tf_op jit(solution)/shard_map/ppermute | solution.py:17
  111.6 7.0 %collective-permute-start.1 = (bf16[2,768]{1,0:T(2,128)(2,1)S(1)}, bf16[2,768]{1,0:T(2,128)(2,1)S(1)}, u32[]{:S(2)}, u32[]{:S(2)}) collective-permute-start(bf16[2,768]{1,0:T(2,128)(2,1)S(1)} %get-tuple-element.123), channel_id=1, source_target_pairs={{1,0},{2,1},{3,2},{4,3},{5,4},{6,5},{7,6},{8,7},{9,8},{10,9},{11,1... | collective-permute-start | bytes 9224 | tf_op jit(solution)/shard_map/ppermute | solution.py:18
  118.8 5.6 %copy-start.4 = (s32[512]{0:T(512)S(1)}, s32[512]{0:T(512)}, u32[]{:S(2)}) copy-start(s32[512]{0:T(512)} %param.27) | copy-start | bytes 6148
  118.8 5.9 %copy-start.3 = (s32[6144,1]{0,1:T(1,128)S(1)}, s32[6144,1]{0,1:T(1,128)}, u32[]{:S(2)}) copy-start(s32[6144,1]{0,1:T(1,128)} %param.28) | copy-start | bytes 73732
  118.9 6.1 %copy-start.7 = (f32[11]{0:T(128)S(1)}, f32[11]{0:T(128)}, u32[]{:S(2)}) copy-start(f32[11]{0:T(128)} %param.29) | copy-start | bytes 136
  118.9 69.1 %copy-start.6 = (f32[768]{0:T(1024)S(1)}, f32[768]{0:T(1024)}, u32[]{:S(2)}) copy-start(f32[768]{0:T(1024)} %param.25) | copy-start | bytes 9220
  124.2 139.9 %reduce-scatter.3.cloned.1.call-start = ((), (), s32[]{:S(2)}) async-start(), calls=%async_computation.4 | async-start | bytes 1253376 | tf_op jit(solution)/shard_map/reduce_scatter | solution.py:146
  187.9 12.2 %copy-start.5 = (bf16[2048,768]{1,0:T(8,128)(2,1)S(1)}, bf16[2048,768]{1,0:T(8,128)(2,1)}, u32[]{:S(2)}) copy-start(bf16[2048,768]{1,0:T(8,128)(2,1)} %all-gather.2.cloned.1.call-done) | copy-start | bytes 9437188
  198.5 1.7 copy-start.8
  203.9 143.3 %reduce-scatter.5.cloned.1.call-start = ((), (), s32[]{:S(2)}) async-start(), calls=%async_computation.5 | async-start | bytes 3538944 | tf_op jit(solution)/shard_map/reduce_scatter | solution.py:152
Sparse Core Ops, SparseCore 0:
  124.3 63.5 all-gather.1
  204.0 60.0 reduce-scatter.2
  268.6 78.5 reduce-scatter.4
